TPU v7x, 128 devices: a whole 4x4x4 slice. The times are simulated.
128 devices in a mesh: group: 8 (over x, z_hi), space: 16 (over y, z_lo, core).
Axes of the slice: x: 4, y: 4, z: 4 (z_hi: 2, z_lo: 2; z = z_hi * 2 + z_lo), core: 2. Of those that a mesh axis runs over, the one named last changes fastest.
Arguments:
- prev_field: float32 [8, 256, 256, 256], P('group', 'space'), may hold values from -6 to 6
- curr_field: float32 [8, 256, 256, 256], P('group', 'space'), may hold values from -6 to 6
- coefficient: float32 [256, 256, 256], P('space'), may hold values from 0.05 to 0.2
- recordings: float32 [8, 2, 512], P('group'), may hold values from -24 to 24
- receivers: int32 [8, 512], P('group'), may hold values from 0 to 16777215
- image_in: float32 [128, 128, 128], P('space', 'group'), may hold values from -6 to 6
Outputs:
- final_field: float32 [8, 256, 256, 256], P('group', 'space')
- image_out: float32 [128, 128, 128], P('space', 'group')
All inputs are finite; a program needn't handle non-finite values.
Results may differ from a plain program's by a relative error of at most 0.00002.
Values sent between devices are 32-bit elements; how exact they have to be, the bound alone decides.
A program may use at most 128 MiB of HBM per device.

v0:
```python
import jax
import jax.numpy as jnp
from jax import lax
from jax.sharding import PartitionSpec as P

STEPS = 2
DEC = 2
COEF = (-205.0 / 72.0, 8.0 / 5.0, -1.0 / 5.0, 8.0 / 315.0, -1.0 / 560.0)


def with_halo(block, sides, width):
    for axis, dim in sides:
        count = lax.axis_size(axis)
        forward = [(i, i + 1) for i in range(count - 1)]
        backward = [(target, source) for source, target in forward]
        low = lax.ppermute(
            lax.slice_in_dim(block, block.shape[dim] - width, None, axis=dim), axis, forward
        )
        high = lax.ppermute(lax.slice_in_dim(block, 0, width, axis=dim), axis, backward)
        block = jnp.concatenate([low, block, high], axis=dim)
    return block


def laplace(zpadded):
    nz = zpadded.shape[0] - 8
    nx = zpadded.shape[1]
    ny = zpadded.shape[2]
    full = jnp.pad(zpadded, ((0, 0), (4, 4), (4, 4)))
    centre = zpadded[4 : 4 + nz]
    total = 3.0 * COEF[0] * centre
    for j in range(1, 5):
        side = zpadded[4 + j : 4 + j + nz] + zpadded[4 - j : 4 - j + nz]
        side = (
            side
            + full[4 : 4 + nz, 4 + j : 4 + j + nx, 4 : 4 + ny]
            + full[4 : 4 + nz, 4 - j : 4 - j + nx, 4 : 4 + ny]
        )
        side = (
            side
            + full[4 : 4 + nz, 4 : 4 + nx, 4 + j : 4 + j + ny]
            + full[4 : 4 + nz, 4 : 4 + nx, 4 - j : 4 - j + ny]
        )
        total = total + COEF[j] * side
    return total


def inject(nxt, coef_planes, first_plane, record_now, index):
    plane_size = nxt.shape[1] * nxt.shape[2]
    planes = nxt.shape[0]
    zpos = index // plane_size - first_plane
    valid = (zpos >= 0) & (zpos < planes)
    local = jnp.where(valid, zpos * plane_size + index % plane_size, 0)
    amount = jnp.where(valid, coef_planes.reshape(-1)[local] * record_now, 0.0)
    return nxt.reshape(-1).at[local].add(amount).reshape(nxt.shape)


def geo_mean(fields):
    return jnp.exp(jnp.mean(jnp.log(1.0 + fields * fields), axis=0)) - 1.0


def on_device(prev_field, curr_field, coefficient, recordings, receivers, image_in):
    prev = prev_field[0]
    curr = curr_field[0]
    record = recordings[0]
    index = receivers[0]
    depth = curr.shape[0]
    slab = lax.axis_index("space")
    for step in range(STEPS):
        padded = with_halo(curr, (("space", 0),), 4)
        nxt = 2.0 * curr - prev + coefficient * laplace(padded)
        nxt = inject(nxt, coefficient, slab * depth, record[step], index)
        prev, curr = (curr, nxt)
    sample = curr[::DEC, ::DEC, ::DEC]
    update = geo_mean(
        lax.all_to_all(sample[None], "group", split_axis=2, concat_axis=0, tiled=True)
    )
    return (curr[None], image_in + update)


def solution(mesh):
    placed = (
        P("group", "space", None, None),
        P("group", "space", None, None),
        P("space", None, None),
        P("group", None, None),
        P("group", None),
        P("space", "group", None),
    )
    return jax.shard_map(
        on_device,
        mesh=mesh,
        in_specs=placed,
        out_specs=(P("group", "space", None, None), P("space", "group", None)),
        check_vma=False,
    )
```

profile of v0, /device:TPU:48, one launch (start us, length us, event | category | flops | bytes accessed | tf_op | source)
XLA Modules:
  0.0 247.5 jit_solution(16478315855580566975)
XLA Ops:
  0.6 2.7 %slice_bitcast_fusion.1 = (f32[4,256,256]{2,1,0:T(8,128)}, f32[4,256,256]{2,1,0:T(8,128)S(1)}) fusion(f32[1,16,256,256]{3,2,1,0:T(8,128)} %param.7), kind=kLoop, calls=%fused_computation.96 | loop fusion | bytes 4194304 | tf_op jit(solution)/shard_map/slice | solution.py:19
  3.3 1.9 collective-permute-start
  5.3 2.4 collective-permute-start.1
  7.7 0.0 copy-start.4
  7.7 0.0 copy-start.5
  7.7 6.4 %copy.13 = f32[512,2,8,128]{3,1,2,0:T(2,128)} copy(f32[512,2,8,128]{3,2,1,0:T(8,128)} %bitcast.41) | data formatting | bytes 8388608
  14.1 0.0 copy-done.4
  14.1 20.1 %gather_fusion = f32[512]{0:T(512)S(1)} fusion(f32[1048576]{0:T(1024)} %bitcast.44, s32[1024]{0:T(1024)S(1)} %pad_clamp_fusion), kind=kCustom, calls=%fused_computation | custom fusion | bytes 6144 | tf_op jit(solution)/shard_map/gather | solution.py:53
  34.2 0.0 copy-done.5
  34.2 0.0 collective-permute-done
  34.2 0.0 collective-permute-done.1
  34.2 8.7 %select_maximum_fusion.2 = f32[24,264,264]{2,1,0:T(8,128)} fusion(f32[4,256,256]{2,1,0:T(8,128)S(1)} %collective-permute-done, f32[16,256,256]{2,1,0:T(8,128)} %bitcast.38, f32[4,256,256]{2,1,0:T(8,128)S(1)} %collective-permute-done.1), kind=kLoop, calls=%fused_computation.9 | loop fusion | flops 25090560 | bytes 12982272 | tf_op jit(solution)/shard_map/concatenate | solution.py:20
  43.0 71.2 %fusion.13 = f32[16,256,256]{2,1,0:T(8,128)} fusion(f32[16,256,256]{2,1,0:T(8,128)} %param.8, f32[16,256,256]{2,1,0:T(8,128)} %bitcast.39, f32[4,256,256]{2,1,0:T(8,128)S(1)} %collective-permute-done.1, f32[4,256,256]{2,1,0:T(8,128)S(1)} %collective-permute-done, f32[24,264,264]{2,1,0:T(8,128)} %select_maximum_fusion.2, f32[1,16,256,256]{3,2,1,0:T(8,128)} %param.6), kind=kLoop, calls=%fused_computation.36 | loop fusion | flops 42991616 | bytes 85983232 | tf_op jit(solution)/shard_map/add | solution.py:70
  114.1 6.3 %copy.12 = f32[512,2,8,128]{3,1,2,0:T(2,128)} copy(f32[512,2,8,128]{3,2,1,0:T(8,128)} %bitcast.43) | data formatting | bytes 8388608
  120.4 8.0 %scatter_fusion = f32[1048576]{0:T(1024)} fusion(f32[1048576]{0:T(1024)} %bitcast.40, s32[512]{0:T(512)S(1)} %bitcast.48, f32[512]{0:T(512)S(1)} %get-tuple-element.11), kind=kCustom, calls=%fused_computation.1 | custom fusion | flops 512 | bytes 8192 | tf_op jit(solution)/shard_map/scatter-add | solution.py:54
  128.4 1.7 fusion.49
  130.1 1.3 slice.244
  131.4 3.5 %collective-permute-start.3 = (f32[4,256,256]{2,1,0:T(8,128)}, f32[4,256,256]{2,1,0:T(8,128)S(1)}, u32[]{:S(2)}, u32[]{:S(2)}) collective-permute-start(f32[4,256,256]{2,1,0:T(8,128)} %slice.244), channel_id=1, source_target_pairs={{0,1},{1,2},{2,3},{3,4},{4,5},{5,6},{6,7},{7,8},{8,9},{9,10},{10,1... | collective-permute-start | bytes 3145736 | tf_op jit(solution)/shard_map/ppermute | solution.py:16
  134.8 0.3 slice.241
  135.1 2.1 collective-permute-start.2
  137.2 5.2 %reshape.178 = f32[16,256,256]{2,1,0:T(8,128)} reshape(f32[1048576]{0:T(1024)} %scatter_fusion) | data formatting | bytes 8388608 | tf_op jit(solution)/shard_map/reshape | solution.py:54
  142.4 16.5 %collective-permute-done.3 = f32[4,256,256]{2,1,0:T(8,128)S(1)} collective-permute-done((f32[4,256,256]{2,1,0:T(8,128)}, f32[4,256,256]{2,1,0:T(8,128)S(1)}, u32[]{:S(2)}, u32[]{:S(2)}) %collective-permute-start.3) | collective-permute-done | bytes 1048608 | tf_op jit(solution)/shard_map/ppermute | solution.py:16
  158.9 0.0 copy-start.2
  158.9 0.1 constant_dynamic-update-slice_fusion.3
  159.0 0.0 copy-start
  159.0 3.6 %constant_dynamic-update-slice_fusion.1 = (f32[20,256,256]{2,1,0:T(8,128)S(1)}, f32[20,256,256]{2,1,0:T(8,128)S(1)}) fusion(f32[16,256,256]{2,1,0:T(8,128)} %reshape.178, f32[20,256,256]{2,1,0:T(8,128)S(1)} %constant_dynamic-update-slice_fusion.3), kind=kLoop, calls=%fused_computation.101 | loop fusion | bytes 12582912
  162.6 0.0 copy-done.2
  162.7 0.0 copy-start.1
  162.7 0.0 collective-permute-done.2
  162.7 0.1 copy-done
  162.8 6.4 %select_maximum_fusion = f32[24,264,264]{2,1,0:T(8,128)S(1)} fusion(f32[4,256,256]{2,1,0:T(8,128)} %collective-permute-done.2, f32[16,256,256]{2,1,0:T(8,128)S(1)} %copy-done, f32[4,256,256]{2,1,0:T(8,128)} %copy-done.2), kind=kLoop, calls=%fused_computation.7 | loop fusion | flops 25090560 | bytes 12982272 | tf_op jit(solution)/shard_map/concatenate | solution.py:20
  169.2 1.3 constant_dynamic-update-slice_fusion
  170.5 0.0 copy-done.1
  170.5 20.0 %fusion.36 = f32[16,256,256]{2,1,0:T(8,128)} fusion(f32[16,256,256]{2,1,0:T(8,128)} %param.8, f32[24,264,264]{2,1,0:T(8,128)S(1)} %select_maximum_fusion, f32[20,256,256]{2,1,0:T(8,128)} %copy-done.1, f32[20,256,256]{2,1,0:T(8,128)S(1)} %constant_dynamic-update-slice_fusion, f32[16,256,256]{2,1,0:T(8,128)S(1)} %copy-done, f32[1,16,256,256]{3,2,1,0:T(8,128)} %param.7), kind=kLoop, calls=%fused_computation.60 | loop fusion | flops 34603008 | bytes 117440512 | tf_op jit(solution)/shard_map/add | solution.py:70
  190.6 6.3 %copy.14 = f32[512,2,8,128]{3,1,2,0:T(2,128)} copy(f32[512,2,8,128]{3,2,1,0:T(8,128)} %bitcast.42) | data formatting | bytes 8388608
  196.8 8.0 %scatter_fusion.1 = f32[1048576]{0:T(1024)} fusion(f32[1048576]{0:T(1024)} %bitcast.37, s32[512]{0:T(512)S(1)} %bitcast.49, f32[512]{0:T(512)S(1)} %get-tuple-element.10), kind=kCustom, calls=%fused_computation.2 | custom fusion | flops 512 | bytes 8192 | tf_op jit(solution)/shard_map/scatter-add | solution.py:54
  204.8 5.2 %reshape.180 = f32[16,256,256]{2,1,0:T(8,128)} reshape(f32[1048576]{0:T(1024)} %scatter_fusion.1) | data formatting | bytes 8388608 | tf_op jit(solution)/shard_map/reshape | solution.py:54
  210.0 18.9 %slice.269 = f32[8,128,128]{2,1,0:T(8,128)S(1)} slice(f32[16,256,256]{2,1,0:T(8,128)} %reshape.180), slice={[0:16:2], [0:256:2], [0:256:2]} | slice | bytes 1048576 | tf_op jit(solution)/shard_map/slice | solution.py:73
  228.9 1.1 copy.9
  230.0 7.0 %all-to-all-start = ((f32[1,8,128,128]{3,1,0,2:T(8,128)}), f32[1,8,128,128]{3,1,0,2:T(8,128)S(1)}, u32[]{:S(2)}, u32[]{:S(2)}) async-start(f32[1,8,128,128]{3,1,0,2:T(8,128)} %copy.9), calls=%async_computation | async-start | bytes 1048576 | tf_op jit(solution)/shard_map/all_to_all | solution.py:75
  237.0 0.0 copy-start.3
  237.0 5.2 %broadcast_in_dim_reshape.3 = f32[1,16,256,256]{3,2,1,0:T(8,128)} reshape(f32[1048576]{0:T(1024)} %scatter_fusion.1) | data formatting | bytes 8388608 | tf_op jit(solution)/shard_map/broadcast_in_dim;reshape | solution.py:77
  242.3 4.5 %all-to-all-done = f32[1,8,128,128]{3,1,0,2:T(8,128)S(1)} async-done(((f32[1,8,128,128]{3,1,0,2:T(8,128)}), f32[1,8,128,128]{3,1,0,2:T(8,128)S(1)}, u32[]{:S(2)}, u32[]{:S(2)}) %all-to-all-start) | async-done | bytes 524320 | tf_op jit(solution)/shard_map/all_to_all | solution.py:75
  246.7 0.1 add_log_fusion
  246.8 0.0 copy-done.3
  246.9 0.6 copy.11
  (6 shorter events, 0.1 us)
Async XLA Ops:
  3.3 30.9 %collective-permute-start = (f32[4,256,256]{2,1,0:T(8,128)}, f32[4,256,256]{2,1,0:T(8,128)S(1)}, u32[]{:S(2)}, u32[]{:S(2)}) collective-permute-start(f32[4,256,256]{2,1,0:T(8,128)} %get-tuple-element.8), channel_id=1, source_target_pairs={{1,0},{2,1},{3,2},{4,3},{5,4},{6,5},{7,6},{8,7},{9,8},{10,9},{11,1... | collective-permute-start | bytes 3145736 | tf_op jit(solution)/shard_map/ppermute | solution.py:19
  5.3 29.0 %collective-permute-start.1 = (f32[4,256,256]{2,1,0:T(8,128)S(1)}, f32[4,256,256]{2,1,0:T(8,128)S(1)}, u32[]{:S(2)}, u32[]{:S(2)}) collective-permute-start(f32[4,256,256]{2,1,0:T(8,128)S(1)} %get-tuple-element.9), channel_id=1, source_target_pairs={{0,1},{1,2},{2,3},{3,4},{4,5},{5,6},{6,7},{7,8},{8,9},{9,10},{10,1... | collective-permute-start | bytes 3145736 | tf_op jit(solution)/shard_map/ppermute | solution.py:16
  7.7 6.4 %copy-start.4 = (s32[1,512]{1,0:T(1,128)S(1)}, s32[1,512]{1,0:T(1,128)}, u32[]{:S(2)}) copy-start(s32[1,512]{1,0:T(1,128)} %param.10) | copy-start | bytes 6148
  7.7 26.5 %copy-start.5 = (f32[1,2,512]{2,1,0:T(2,128)S(1)}, f32[1,2,512]{2,1,0:T(2,128)}, u32[]{:S(2)}) copy-start(f32[1,2,512]{2,1,0:T(2,128)} %param.9) | copy-start | bytes 12292
  131.4 27.6 %collective-permute-start.3 = (f32[4,256,256]{2,1,0:T(8,128)}, f32[4,256,256]{2,1,0:T(8,128)S(1)}, u32[]{:S(2)}, u32[]{:S(2)}) collective-permute-start(f32[4,256,256]{2,1,0:T(8,128)} %slice.244), channel_id=1, source_target_pairs={{0,1},{1,2},{2,3},{3,4},{4,5},{5,6},{6,7},{7,8},{8,9},{9,10},{10,1... | collective-permute-start | bytes 3145736 | tf_op jit(solution)/shard_map/ppermute | solution.py:16
  135.1 27.5 %collective-permute-start.2 = (f32[4,256,256]{2,1,0:T(8,128)S(1)}, f32[4,256,256]{2,1,0:T(8,128)}, u32[]{:S(2)}, u32[]{:S(2)}) collective-permute-start(f32[4,256,256]{2,1,0:T(8,128)S(1)} %slice.241), channel_id=1, source_target_pairs={{1,0},{2,1},{3,2},{4,3},{5,4},{6,5},{7,6},{8,7},{9,8},{10,9},{11,1... | collective-permute-start | bytes 3145736 | tf_op jit(solution)/shard_map/ppermute | solution.py:19
  158.9 3.7 %copy-start.2 = (f32[4,256,256]{2,1,0:T(8,128)}, f32[4,256,256]{2,1,0:T(8,128)S(1)}, u32[]{:S(2)}) copy-start(f32[4,256,256]{2,1,0:T(8,128)S(1)} %collective-permute-done.3) | copy-start | bytes 3145732
  159.0 3.8 %copy-start = (f32[16,256,256]{2,1,0:T(8,128)S(1)}, f32[16,256,256]{2,1,0:T(8,128)}, u32[]{:S(2)}) copy-start(f32[16,256,256]{2,1,0:T(8,128)} %reshape.178) | copy-start | bytes 12582916
  162.7 7.9 %copy-start.1 = (f32[20,256,256]{2,1,0:T(8,128)}, f32[20,256,256]{2,1,0:T(8,128)S(1)}, u32[]{:S(2)}) copy-start(f32[20,256,256]{2,1,0:T(8,128)S(1)} %get-tuple-element.5) | copy-start | bytes 15728644
  230.0 16.7 %all-to-all-start = ((f32[1,8,128,128]{3,1,0,2:T(8,128)}), f32[1,8,128,128]{3,1,0,2:T(8,128)S(1)}, u32[]{:S(2)}, u32[]{:S(2)}) async-start(f32[1,8,128,128]{3,1,0,2:T(8,128)} %copy.9), calls=%async_computation | async-start | bytes 1048576 | tf_op jit(solution)/shard_map/all_to_all | solution.py:75
  237.0 9.8 %copy-start.3 = (f32[8,16,128]{2,1,0:T(8,128)S(1)}, f32[8,16,128]{2,1,0:T(8,128)}, u32[]{:S(2)}) copy-start(f32[8,16,128]{2,1,0:T(8,128)} %param.11) | copy-start | bytes 196612
where the time goes:
time: 249 us; the launch traced here: 248 us
  other arithmetic  123 us (49%)
  local copies, waits for them, and re-layouts  86.2 us (35%)
  waiting for transfers between devices  21 us (8%)
  starting transfers between devices  16.9 us (7%)
    add x2, other arithmetic, on_device(): nxt = 2.0 * curr - prev + coefficient * laplace(padded)  91.2 us
    unnamed x18, local copies, waits for them, and re-layouts  23.4 us
    gather x1, local copies, waits for them, and re-layouts, inject(): amount = jnp.where(valid, coef_planes.reshape(-1)[local] * record_now, 0.0)  20.1 us
    slice x1, local copies, waits for them, and re-layouts, on_device(): sample = curr[::DEC, ::DEC, ::DEC]  18.9 us
    ppermute x2, waiting for transfers between devices, with_halo(): lax.ppermute(lax.slice_in_dim(block, block.shape[dim] - width, None, axis...  16.5 us
    scatter-add x2, other arithmetic, inject(): return nxt.reshape(-1).at[local].add(amount).reshape(nxt.shape)  16 us
    concatenate x2, other arithmetic, with_halo(): block = jnp.concatenate([low, block, high], axis=dim)  15.2 us
    reshape x2, local copies, waits for them, and re-layouts, inject(): return nxt.reshape(-1).at[local].add(amount).reshape(nxt.shape)  10.4 us
  transfers between devices with their start and end apart: 5, of which 2 were waited for; matrix products, arithmetic and copies ran while one was open for 17% of the time, Pallas kernels for 0%

commit v1 on v0

--- a/solution.py
+++ b/solution.py
@@ -72,7 +72,15 @@
         prev, curr = (curr, nxt)
     sample = curr[::DEC, ::DEC, ::DEC]
     update = geo_mean(
-        lax.all_to_all(sample[None], "group", split_axis=2, concat_axis=0, tiled=True)
+        jnp.concatenate(
+            jax.lax.all_to_all(
+                jnp.stack(jnp.split(sample[None], jax.lax.axis_size("group"), axis=2)),
+                axis_name="group",
+                split_axis=0,
+                concat_axis=0,
+            ),
+            axis=0,
+        )
     )
     return (curr[None], image_in + update)
 

time: 249 us -> 253 us (1.016)
  local copies, waits for them, and re-layouts: 86.2 us -> 89.5 us
    unnamed x18 -> x24, local copies, waits for them, and re-layouts: 23.4 us -> 27.1 us
  transfers between devices with their start and end apart: 5 -> 5, of which waited for: 2 -> 2; matrix products, arithmetic and copies ran while one was open for 17% -> 16% of each run, Pallas kernels for 0% -> 0%
where the time goes in v1:
time: 253 us; the launch traced here: 251 us
  other arithmetic  123 us (49%)
  local copies, waits for them, and re-layouts  89.5 us (35%)
  waiting for transfers between devices  21 us (8%)
  starting transfers between devices  16.9 us (7%)
    add x2, other arithmetic, on_device(): nxt = 2.0 * curr - prev + coefficient * laplace(padded)  91.2 us
    unnamed x24, local copies, waits for them, and re-layouts  27.1 us
    gather x1, local copies, waits for them, and re-layouts, inject(): amount = jnp.where(valid, coef_planes.reshape(-1)[local] * record_now, 0.0)  20.1 us
    slice x1, local copies, waits for them, and re-layouts, on_device(): sample = curr[::DEC, ::DEC, ::DEC]  18.9 us
    ppermute x2, waiting for transfers between devices, with_halo(): lax.ppermute(lax.slice_in_dim(block, block.shape[dim] - width, None, axis...  16.5 us
    scatter-add x2, other arithmetic, inject(): return nxt.reshape(-1).at[local].add(amount).reshape(nxt.shape)  16 us
    concatenate x2, other arithmetic, with_halo(): block = jnp.concatenate([low, block, high], axis=dim)  15.2 us
    reshape x2, local copies, waits for them, and re-layouts, inject(): return nxt.reshape(-1).at[local].add(amount).reshape(nxt.shape)  10.4 us
  transfers between devices with their start and end apart: 5, of which 2 were waited for; matrix products, arithmetic and copies ran while one was open for 16% of the time, Pallas kernels for 0%

profile of v1, /device:TPU:48, one launch (start us, length us, event | category | flops | bytes accessed | tf_op | source)
XLA Modules:
  0.0 251.4 jit_solution(16184973800624710082)
XLA Ops:
  0.6 2.7 %slice_bitcast_fusion.1 = (f32[4,256,256]{2,1,0:T(8,128)}, f32[4,256,256]{2,1,0:T(8,128)S(1)}) fusion(f32[1,16,256,256]{3,2,1,0:T(8,128)} %param.7), kind=kLoop, calls=%fused_computation.96 | loop fusion | bytes 4194304 | tf_op jit(solution)/shard_map/slice | solution.py:19
  3.3 1.9 collective-permute-start
  5.3 2.4 collective-permute-start.1
  7.7 0.0 copy-start.4
  7.7 0.0 copy-start.5
  7.7 6.4 %copy.9 = f32[512,2,8,128]{3,1,2,0:T(2,128)} copy(f32[512,2,8,128]{3,2,1,0:T(8,128)} %bitcast.72) | data formatting | bytes 8388608
  14.1 0.0 copy-done.4
  14.1 20.1 %gather_fusion = f32[512]{0:T(512)S(1)} fusion(f32[1048576]{0:T(1024)} %bitcast.75, s32[1024]{0:T(1024)S(1)} %pad_clamp_fusion), kind=kCustom, calls=%fused_computation | custom fusion | bytes 6144 | tf_op jit(solution)/shard_map/gather | solution.py:53
  34.2 0.0 copy-done.5
  34.2 0.0 collective-permute-done
  34.2 0.0 collective-permute-done.1
  34.2 8.7 %select_maximum_fusion.2 = f32[24,264,264]{2,1,0:T(8,128)} fusion(f32[4,256,256]{2,1,0:T(8,128)S(1)} %collective-permute-done, f32[16,256,256]{2,1,0:T(8,128)} %bitcast.69, f32[4,256,256]{2,1,0:T(8,128)S(1)} %collective-permute-done.1), kind=kLoop, calls=%fused_computation.9 | loop fusion | flops 25090560 | bytes 12982272 | tf_op jit(solution)/shard_map/concatenate | solution.py:20
  43.0 71.2 %fusion.13 = f32[16,256,256]{2,1,0:T(8,128)} fusion(f32[16,256,256]{2,1,0:T(8,128)} %param.8, f32[16,256,256]{2,1,0:T(8,128)} %bitcast.70, f32[4,256,256]{2,1,0:T(8,128)S(1)} %collective-permute-done.1, f32[4,256,256]{2,1,0:T(8,128)S(1)} %collective-permute-done, f32[24,264,264]{2,1,0:T(8,128)} %select_maximum_fusion.2, f32[1,16,256,256]{3,2,1,0:T(8,128)} %param.6), kind=kLoop, calls=%fused_computation.36 | loop fusion | flops 42991616 | bytes 85983232 | tf_op jit(solution)/shard_map/add | solution.py:70
  114.1 6.3 %copy.8 = f32[512,2,8,128]{3,1,2,0:T(2,128)} copy(f32[512,2,8,128]{3,2,1,0:T(8,128)} %bitcast.74) | data formatting | bytes 8388608
  120.4 8.0 %scatter_fusion = f32[1048576]{0:T(1024)} fusion(f32[1048576]{0:T(1024)} %bitcast.71, s32[512]{0:T(512)S(1)} %bitcast.85, f32[512]{0:T(512)S(1)} %get-tuple-element.9), kind=kCustom, calls=%fused_computation.1 | custom fusion | flops 512 | bytes 8192 | tf_op jit(solution)/shard_map/scatter-add | solution.py:54
  128.4 1.7 fusion.57
  130.1 1.3 slice.244
  131.4 3.5 %collective-permute-start.3 = (f32[4,256,256]{2,1,0:T(8,128)}, f32[4,256,256]{2,1,0:T(8,128)S(1)}, u32[]{:S(2)}, u32[]{:S(2)}) collective-permute-start(f32[4,256,256]{2,1,0:T(8,128)} %slice.244), channel_id=1, source_target_pairs={{0,1},{1,2},{2,3},{3,4},{4,5},{5,6},{6,7},{7,8},{8,9},{9,10},{10,1... | collective-permute-start | bytes 3145736 | tf_op jit(solution)/shard_map/ppermute | solution.py:16
  134.8 0.3 slice.241
  135.1 2.1 collective-permute-start.2
  137.2 5.2 %reshape.176 = f32[16,256,256]{2,1,0:T(8,128)} reshape(f32[1048576]{0:T(1024)} %scatter_fusion) | data formatting | bytes 8388608 | tf_op jit(solution)/shard_map/reshape | solution.py:54
  142.4 16.5 %collective-permute-done.3 = f32[4,256,256]{2,1,0:T(8,128)S(1)} collective-permute-done((f32[4,256,256]{2,1,0:T(8,128)}, f32[4,256,256]{2,1,0:T(8,128)S(1)}, u32[]{:S(2)}, u32[]{:S(2)}) %collective-permute-start.3) | collective-permute-done | bytes 1048608 | tf_op jit(solution)/shard_map/ppermute | solution.py:16
  158.9 0.0 copy-start.2
  158.9 0.1 constant_dynamic-update-slice_fusion.3
  159.0 0.0 copy-start
  159.0 3.6 %constant_dynamic-update-slice_fusion.1 = (f32[20,256,256]{2,1,0:T(8,128)S(1)}, f32[20,256,256]{2,1,0:T(8,128)S(1)}) fusion(f32[16,256,256]{2,1,0:T(8,128)} %reshape.176, f32[20,256,256]{2,1,0:T(8,128)S(1)} %constant_dynamic-update-slice_fusion.3), kind=kLoop, calls=%fused_computation.116 | loop fusion | bytes 12582912
  162.6 0.0 copy-done.2
  162.7 0.0 copy-start.1
  162.7 0.0 collective-permute-done.2
  162.7 0.1 copy-done
  162.8 6.4 %select_maximum_fusion = f32[24,264,264]{2,1,0:T(8,128)S(1)} fusion(f32[4,256,256]{2,1,0:T(8,128)} %collective-permute-done.2, f32[16,256,256]{2,1,0:T(8,128)S(1)} %copy-done, f32[4,256,256]{2,1,0:T(8,128)} %copy-done.2), kind=kLoop, calls=%fused_computation.7 | loop fusion | flops 25090560 | bytes 12982272 | tf_op jit(solution)/shard_map/concatenate | solution.py:20
  169.2 1.3 constant_dynamic-update-slice_fusion
  170.5 0.0 copy-done.1
  170.5 20.0 %fusion.36 = f32[16,256,256]{2,1,0:T(8,128)} fusion(f32[16,256,256]{2,1,0:T(8,128)} %param.8, f32[24,264,264]{2,1,0:T(8,128)S(1)} %select_maximum_fusion, f32[20,256,256]{2,1,0:T(8,128)} %copy-done.1, f32[20,256,256]{2,1,0:T(8,128)S(1)} %constant_dynamic-update-slice_fusion, f32[16,256,256]{2,1,0:T(8,128)S(1)} %copy-done, f32[1,16,256,256]{3,2,1,0:T(8,128)} %param.7), kind=kLoop, calls=%fused_computation.60 | loop fusion | flops 34603008 | bytes 117440512 | tf_op jit(solution)/shard_map/add | solution.py:70
  190.6 6.3 %copy.10 = f32[512,2,8,128]{3,1,2,0:T(2,128)} copy(f32[512,2,8,128]{3,2,1,0:T(8,128)} %bitcast.73) | data formatting | bytes 8388608
  196.8 8.0 %scatter_fusion.1 = f32[1048576]{0:T(1024)} fusion(f32[1048576]{0:T(1024)} %bitcast.68, s32[512]{0:T(512)S(1)} %bitcast.86, f32[512]{0:T(512)S(1)} %get-tuple-element.8), kind=kCustom, calls=%fused_computation.2 | custom fusion | flops 512 | bytes 8192 | tf_op jit(solution)/shard_map/scatter-add | solution.py:54
  204.8 5.2 %reshape.178 = f32[16,256,256]{2,1,0:T(8,128)} reshape(f32[1048576]{0:T(1024)} %scatter_fusion.1) | data formatting | bytes 8388608 | tf_op jit(solution)/shard_map/reshape | solution.py:54
  210.0 18.9 %slice.269 = f32[8,128,128]{2,1,0:T(8,128)S(1)} slice(f32[16,256,256]{2,1,0:T(8,128)} %reshape.178), slice={[0:16:2], [0:256:2], [0:256:2]} | slice | bytes 1048576 | tf_op jit(solution)/shard_map/slice | solution.py:73
  228.9 0.6 fusion.52
  229.5 0.6 fusion.51
  230.1 0.6 fusion.50
  230.7 0.6 fusion.49
  231.4 0.6 fusion.48
  232.0 0.6 fusion.47
  232.6 0.6 fusion.46
  233.3 0.6 fusion.45
  233.9 7.0 %all-to-all-start = ((f32[8,1,8,16,128]{4,3,2,1,0:T(8,128)}), f32[8,1,8,16,128]{4,3,2,1,0:T(8,128)S(1)}, u32[]{:S(2)}, u32[]{:S(2)}) async-start(f32[8,1,8,16,128]{4,3,2,1,0:T(8,128)} %fusion.45), calls=%async_computation | async-start | bytes 1048576 | tf_op jit(solution)/shard_map/all_to_all | solution.py:76
  241.0 0.0 copy-start.3
  241.0 5.2 %broadcast_in_dim_reshape.3 = f32[1,16,256,256]{3,2,1,0:T(8,128)} reshape(f32[1048576]{0:T(1024)} %scatter_fusion.1) | data formatting | bytes 8388608 | tf_op jit(solution)/shard_map/broadcast_in_dim;reshape | solution.py:85
  246.2 4.5 %all-to-all-done = f32[8,1,8,16,128]{4,3,2,1,0:T(8,128)S(1)} async-done(((f32[8,1,8,16,128]{4,3,2,1,0:T(8,128)}), f32[8,1,8,16,128]{4,3,2,1,0:T(8,128)S(1)}, u32[]{:S(2)}, u32[]{:S(2)}) %all-to-all-start) | async-done | bytes 524320 | tf_op jit(solution)/shard_map/all_to_all | solution.py:76
  250.6 0.1 log_reduce_fusion
  250.7 0.0 copy-done.3
  250.8 0.6 add_add_fusion
  (4 shorter events, 0.1 us)
Async XLA Ops:
  3.3 30.9 %collective-permute-start = (f32[4,256,256]{2,1,0:T(8,128)}, f32[4,256,256]{2,1,0:T(8,128)S(1)}, u32[]{:S(2)}, u32[]{:S(2)}) collective-permute-start(f32[4,256,256]{2,1,0:T(8,128)} %get-tuple-element.6), channel_id=1, source_target_pairs={{1,0},{2,1},{3,2},{4,3},{5,4},{6,5},{7,6},{8,7},{9,8},{10,9},{11,1... | collective-permute-start | bytes 3145736 | tf_op jit(solution)/shard_map/ppermute | solution.py:19
  5.3 29.0 %collective-permute-start.1 = (f32[4,256,256]{2,1,0:T(8,128)S(1)}, f32[4,256,256]{2,1,0:T(8,128)S(1)}, u32[]{:S(2)}, u32[]{:S(2)}) collective-permute-start(f32[4,256,256]{2,1,0:T(8,128)S(1)} %get-tuple-element.7), channel_id=1, source_target_pairs={{0,1},{1,2},{2,3},{3,4},{4,5},{5,6},{6,7},{7,8},{8,9},{9,10},{10,1... | collective-permute-start | bytes 3145736 | tf_op jit(solution)/shard_map/ppermute | solution.py:16
  7.7 6.4 %copy-start.4 = (s32[1,512]{1,0:T(1,128)S(1)}, s32[1,512]{1,0:T(1,128)}, u32[]{:S(2)}) copy-start(s32[1,512]{1,0:T(1,128)} %param.10) | copy-start | bytes 6148
  7.7 26.5 %copy-start.5 = (f32[1,2,512]{2,1,0:T(2,128)S(1)}, f32[1,2,512]{2,1,0:T(2,128)}, u32[]{:S(2)}) copy-start(f32[1,2,512]{2,1,0:T(2,128)} %param.9) | copy-start | bytes 12292
  131.4 27.6 %collective-permute-start.3 = (f32[4,256,256]{2,1,0:T(8,128)}, f32[4,256,256]{2,1,0:T(8,128)S(1)}, u32[]{:S(2)}, u32[]{:S(2)}) collective-permute-start(f32[4,256,256]{2,1,0:T(8,128)} %slice.244), channel_id=1, source_target_pairs={{0,1},{1,2},{2,3},{3,4},{4,5},{5,6},{6,7},{7,8},{8,9},{9,10},{10,1... | collective-permute-start | bytes 3145736 | tf_op jit(solution)/shard_map/ppermute | solution.py:16
  135.1 27.5 %collective-permute-start.2 = (f32[4,256,256]{2,1,0:T(8,128)S(1)}, f32[4,256,256]{2,1,0:T(8,128)}, u32[]{:S(2)}, u32[]{:S(2)}) collective-permute-start(f32[4,256,256]{2,1,0:T(8,128)S(1)} %slice.241), channel_id=1, source_target_pairs={{1,0},{2,1},{3,2},{4,3},{5,4},{6,5},{7,6},{8,7},{9,8},{10,9},{11,1... | collective-permute-start | bytes 3145736 | tf_op jit(solution)/shard_map/ppermute | solution.py:19
  158.9 3.7 %copy-start.2 = (f32[4,256,256]{2,1,0:T(8,128)}, f32[4,256,256]{2,1,0:T(8,128)S(1)}, u32[]{:S(2)}) copy-start(f32[4,256,256]{2,1,0:T(8,128)S(1)} %collective-permute-done.3) | copy-start | bytes 3145732
  159.0 3.8 %copy-start = (f32[16,256,256]{2,1,0:T(8,128)S(1)}, f32[16,256,256]{2,1,0:T(8,128)}, u32[]{:S(2)}) copy-start(f32[16,256,256]{2,1,0:T(8,128)} %reshape.176) | copy-start | bytes 12582916
  162.7 7.9 %copy-start.1 = (f32[20,256,256]{2,1,0:T(8,128)}, f32[20,256,256]{2,1,0:T(8,128)S(1)}, u32[]{:S(2)}) copy-start(f32[20,256,256]{2,1,0:T(8,128)S(1)} %get-tuple-element.3) | copy-start | bytes 15728644
  233.9 16.7 %all-to-all-start = ((f32[8,1,8,16,128]{4,3,2,1,0:T(8,128)}), f32[8,1,8,16,128]{4,3,2,1,0:T(8,128)S(1)}, u32[]{:S(2)}, u32[]{:S(2)}) async-start(f32[8,1,8,16,128]{4,3,2,1,0:T(8,128)} %fusion.45), calls=%async_computation | async-start | bytes 1048576 | tf_op jit(solution)/shard_map/all_to_all | solution.py:76
  241.0 9.8 %copy-start.3 = (f32[8,16,128]{2,1,0:T(8,128)S(1)}, f32[8,16,128]{2,1,0:T(8,128)}, u32[]{:S(2)}) copy-start(f32[8,16,128]{2,1,0:T(8,128)} %param.11) | copy-start | bytes 196612
